TPU v7x, 256 devices: a 8x8x2 block of a 8x8x16 slice. The times are simulated.
256 devices in a mesh: grp: 2 (over z), tp: 128 (over y, x, core).
Axes of the slice: x: 8, y: 8, z: 2, core: 2. Of those that a mesh axis runs over, the one named last changes fastest.
The devices are a block of a 8x8x16 slice.
Arguments:
- hidden: bfloat16 [1024, 16384], P('grp', 'tp'), parts along dimension 0, may hold values from -36 to 36
- norm_gain: float32 [16384], P('tp'), may hold values from 0.3 to 10, as said below
- prefix: int32 [2], P('grp'), parts along dimension 0, may hold values from 0 to 8192
- w_query: bfloat16 [16384, 16384], P(None, 'tp'), may hold values from -0.046875 to 0.046875
- w_kv: bfloat16 [2048, 16384], P('tp'), may hold values from -0.046875 to 0.046875
- w_scale: float32 [18432], P('tp'), may hold values from 0.25 to 4
Outputs:
- queries: bfloat16 [1024, 16384], P('grp', 'tp'), parts along dimension 0
- keys: bfloat16 [1024, 16384], P('grp', 'tp'), parts along dimension 0
- values: bfloat16 [1024, 16384], P('grp', 'tp'), parts along dimension 0
- payload: bfloat16 [1024, 16384], P('grp', 'tp'), parts along dimension 0
- row_scale: float32 [1024], P('grp'), parts along dimension 0
There are 2 independent parts, one for each index of `grp`. A program takes and returns all parts, laid end to end along the dimension named above; an argument that names none is the same for every part. Nothing has to cross between parts.
Inputs may be any that keep to these rules, and one draw needn't show every extreme that they name: `norm_gain`: positive.
All inputs are finite; a program needn't handle non-finite values. Where the computation divides by a largest or mean magnitude, that divisor is 1e-20 or more.
Results may differ from a plain program's by a relative error of at most 0.012.
Values may be sent and summed in bfloat16 or wider, within the bound.
A program may use at most 64 MiB of HBM per device.

v0:
```python
import jax
import jax.numpy as jnp
from jax import lax
from jax.sharding import PartitionSpec as P

D = 16384
HD = 128
HQ_DEV = 1
KV_COLS_DEV = 8
norm_eps = 1e-05
tiny_eps = 1e-06
rope_base = 500000.0


def turned_gather(arrays, axis, dims):
    turned = [jnp.moveaxis(a, dim, 0) for a, dim in zip(arrays, dims)]
    widths = [t[0].size for t in turned]
    both = jnp.concatenate([t.reshape(-1, w) for t, w in zip(turned, widths)], axis=1)
    whole = lax.all_gather(both, axis, axis=0, tiled=True)
    blocks = jnp.split(whole, [sum(widths[:k]) for k in range(1, len(widths))], axis=1)
    return tuple(
        (
            jnp.moveaxis(b.reshape(-1, *t.shape[1:]), 0, dim)
            for b, t, dim in zip(blocks, turned, dims)
        )
    )


def rotate(matrix, positions, offset):
    count, width = matrix.shape
    pairs = matrix.reshape(count, width // 2, 2)
    columns = offset + 2 * jnp.arange(width // 2, dtype=jnp.int32)
    pair_index = (columns % HD // 2).astype(jnp.float32)
    inverse_freq = jnp.power(jnp.float32(rope_base), -(2.0 * pair_index) / HD)
    angle = positions.astype(jnp.float32)[:, None] * inverse_freq[None, :]
    cosine = jnp.cos(angle)
    sine = jnp.sin(angle)
    first = pairs[:, :, 0]
    second = pairs[:, :, 1]
    turned = jnp.stack([first * cosine - second * sine, second * cosine + first * sine], axis=-1)
    return turned.reshape(count, width)


def kv_product(left, right_rows):
    return lax.dot_general(
        left, right_rows, (((1,), (1,)), ((), ())), preferred_element_type=jnp.float32
    )


def pick_head(gathered, head, kv_heads):
    count = gathered.shape[0]
    pieces = gathered.shape[1] // (kv_heads * KV_COLS_DEV)
    grouped = gathered.reshape(count, pieces, kv_heads, KV_COLS_DEV)
    chosen = lax.dynamic_slice_in_dim(grouped, head, 1, 2)
    return chosen.reshape(count, pieces * KV_COLS_DEV)


def local(hidden, norm_gain, prefix, w_query, w_kv, w_scale):
    count = hidden.shape[0]
    local_width = hidden.shape[1]
    whole, gains = (
        lax.all_gather(hidden, "tp", axis=1, tiled=True),
        lax.all_gather(norm_gain[None, :].astype(jnp.bfloat16), "tp", axis=1, tiled=True).astype(
            jnp.float32
        ),
    )
    widened = whole.astype(jnp.float32)
    square_sum = jnp.sum(widened * widened, axis=1)
    inverse = 1.0 / jnp.sqrt(square_sum / D + norm_eps)
    normed = widened * gains * inverse[:, None]
    row_scale = jnp.max(jnp.abs(normed), axis=1) + tiny_eps
    full_payload = (normed / row_scale[:, None]).astype(jnp.bfloat16)
    payload = lax.dynamic_slice_in_dim(
        full_payload, lax.axis_index("tp") * local_width, local_width, 1
    )
    query_raw = jnp.dot(full_payload, w_query, preferred_element_type=jnp.float32)
    kv_raw = kv_product(full_payload, w_kv)
    proj = jnp.concatenate([query_raw, kv_raw], axis=1)
    proj = proj * row_scale[:, None] * w_scale[None, :]
    qwidth = HQ_DEV * HD
    query_cols = proj[:, :qwidth]
    key_cols = proj[:, qwidth : qwidth + KV_COLS_DEV]
    value_cols = proj[:, qwidth + KV_COLS_DEV :]
    kv_heads = KV_COLS_DEV * lax.axis_size("tp") // HD
    my_index = lax.axis_index("tp")
    positions = prefix[0] + jnp.arange(count, dtype=jnp.int32)
    queries = rotate(query_cols, positions, 0).astype(jnp.bfloat16)
    rotated_keys = rotate(key_cols, positions, my_index // kv_heads * KV_COLS_DEV).astype(
        jnp.bfloat16
    )
    value_round = value_cols.astype(jnp.bfloat16)
    all_keys, all_values = turned_gather((rotated_keys, value_round), "tp", (1, 1))
    head = my_index * kv_heads // lax.axis_size("tp")
    key_head = pick_head(all_keys, head, kv_heads)
    value_head = pick_head(all_values, head, kv_heads)
    keys = jnp.tile(key_head, (1, HQ_DEV))
    values = jnp.tile(value_head, (1, HQ_DEV))
    return (queries, keys, values, payload, row_scale)


def solution(mesh):
    return jax.shard_map(
        local,
        mesh=mesh,
        in_specs=(P("grp", "tp"), P("tp"), P("grp"), P(None, "tp"), P("tp", None), P("tp")),
        out_specs=(P("grp", "tp"), P("grp", "tp"), P("grp", "tp"), P("grp", "tp"), P("grp")),
        check_vma=False,
    )
```

profile of v0, /device:TPU:513, one launch (start us, length us, event | category | flops | bytes accessed | tf_op | source)
XLA Modules:
  0.0 265.4 jit_solution(17900371330747141451)
XLA Ops:
  7.2 0.0 copy-start
  7.2 0.1 all-gather.5.cloned.1.call-start
  7.3 0.7 all-gather.5.cloned.1.call-update
  8.0 0.1 all-gather.7.cloned.1.call-start
  8.1 0.7 convert_bitcast_fusion
  8.7 58.2 %all-gather.1 = bf16[128,1,128]{2,1,0:T(2,128)(2,1)S(1)} all-gather(bf16[1,1,128]{2,1,0:T(2,128)(2,1)S(1)} %convert_bitcast_fusion), channel_id=2, replica_groups=mesh['grp'=2,'tp'=128] {'tp'}, dimensions={0}, use_global_device_ids=true | all-gather | bytes 33024 | tf_op jit(solution)/shard_map/all_gather | solution.py:63
  66.9 0.1 mul.199
  67.7 68.7 %all-gather.5.cloned.1.call-done = bf16[512,16384]{1,0:T(8,128)(2,1)} async-done(((bf16[512,128]{1,0:T(8,128)(2,1)}), bf16[512,16384]{1,0:T(8,128)(2,1)}) %all-gather.5.cloned.1.call-update) | async-done | bytes 16777232 | tf_op jit(solution)/shard_map/all_gather | solution.py:62
  136.3 7.4 %fusion.5 = f32[512]{0:T(512)S(1)} fusion(bf16[512,16384]{1,0:T(8,128)(2,1)} %all-gather.5.cloned.1.call-done), kind=kLoop, calls=%fused_computation.7 | loop fusion | flops 25165312 | bytes 16779264 | tf_op jit(solution)/shard_map/reduce_sum | solution.py:68
  143.8 3.2 %copy-done.2 = bf16[512,16384]{1,0:T(8,128)(2,1)S(1)} copy-done((bf16[512,16384]{1,0:T(8,128)(2,1)S(1)}, bf16[512,16384]{1,0:T(8,128)(2,1)}, u32[]{:S(2)}) %copy-start.2) | copy-done | bytes 16777240
  147.0 6.2 %fusion.3 = f32[512]{0:T(512)S(1)} fusion(bf16[512,16384]{1,0:T(8,128)(2,1)S(1)} %copy-done.2, f32[16384]{0:T(1024)S(1)} %bitcast.36, f32[512]{0:T(512)S(1)} %add_rsqrt_fusion), kind=kLoop, calls=%fused_computation.5 | loop fusion | flops 41942528 | bytes 16846848 | tf_op jit(solution)/shard_map/reduce_max | solution.py:71
  153.2 0.0 copy-start.4
  153.2 5.5 %fusion.4 = bf16[512,16384]{1,0:T(8,128)(2,1)S(1)} fusion(bf16[512,16384]{1,0:T(8,128)(2,1)S(1)} %copy-done.2, f32[16384]{0:T(1024)S(1)} %bitcast.37, f32[512]{0:T(512)S(1)} %broadcast_add_fusion, f32[512]{0:T(512)S(1)} %add_rsqrt_fusion), kind=kLoop, calls=%fused_computation.6 | loop fusion | flops 41943040 | bytes 33624064 | tf_op jit(solution)/shard_map/convert_element_type | solution.py:72
  158.7 0.0 copy-start.1
  158.7 5.7 %copy-done.1 = bf16[512,16384]{1,0:T(8,128)(2,1)} copy-done((bf16[512,16384]{1,0:T(8,128)(2,1)}, bf16[512,16384]{1,0:T(8,128)(2,1)S(1)}, u32[]{:S(2)}) %copy-start.1) | copy-done | bytes 16777240
  164.5 4.4 %fusion.30 = f32[512,16]{0,1:T(8,128)S(1)} fusion(bf16[512,16384]{1,0:T(8,128)(2,1)S(1)} %fusion.4, bf16[16,16384]{1,0:T(8,128)(2,1)S(1)} %copy-done), kind=kOutput, calls=%fused_computation.64 | convolution fusion | flops 268435456 | bytes 17334272 | tf_op jit(solution)/shard_map/dot_general | solution.py:45
  168.9 9.3 %fusion.29 = f32[512,128]{0,1:T(8,128)S(1)} fusion(bf16[512,16384]{1,0:T(8,128)(2,1)} %copy-done.1, bf16[16384,128]{1,0:T(8,128)(2,1)S(1)} %copy-done.3), kind=kOutput, calls=%fused_computation.63 | convolution fusion | flops 2147483648 | bytes 21233664 | tf_op jit(solution)/shard_map/dot_general | solution.py:76
  178.2 0.1 fusion.6
  178.3 0.1 fusion.20
  178.5 0.6 pad_maximum_fusion.1
  179.1 0.1 all-gather.7.cloned.1.call-update
  179.3 0.1 reshape.290
  179.4 0.2 fusion.27
  179.6 0.6 fusion.12
  180.2 0.1 copy.32
  180.4 0.1 convert_element_type.50
  180.4 0.8 copy.38
  181.2 1.6 constant_dynamic-slice_fusion
  182.8 72.5 %all-gather.7.cloned.1.call-done = bf16[1024,1024]{1,0:T(8,128)(2,1)} async-done(((bf16[8,1024]{1,0:T(8,128)(2,1)}), bf16[1024,1024]{1,0:T(8,128)(2,1)}) %all-gather.7.cloned.1.call-update) | async-done | bytes 2097168 | tf_op jit(solution)/shard_map/all_gather | solution.py:19
  255.3 1.7 fusion.26
  257.0 0.8 copy.39
  257.7 0.8 copy.40
  (22 shorter events, 0.2 us)
Async XLA Ops:
  7.2 157.3 %copy-start = (bf16[16,16384]{1,0:T(8,128)(2,1)S(1)}, bf16[16,16384]{1,0:T(8,128)(2,1)}, u32[]{:S(2)}) copy-start(bf16[16,16384]{1,0:T(8,128)(2,1)} %param.10) | copy-start | bytes 1572868
  7.2 129.1 %all-gather.5.cloned.1.call-start = ((), (), s32[]{:S(2)}) async-start(), calls=%async_computation | async-start | bytes 16908288 | tf_op jit(solution)/shard_map/all_gather | solution.py:62
  8.0 247.3 %all-gather.7.cloned.1.call-start = ((), (), s32[]{:S(2)}) async-start(), calls=%async_computation.1 | async-start | bytes 2113536 | tf_op jit(solution)/shard_map/all_gather | solution.py:19
  136.3 10.7 %copy-start.2 = (bf16[512,16384]{1,0:T(8,128)(2,1)S(1)}, bf16[512,16384]{1,0:T(8,128)(2,1)}, u32[]{:S(2)}) copy-start(bf16[512,16384]{1,0:T(8,128)(2,1)} %all-gather.5.cloned.1.call-done) | copy-start | bytes 50331652
  153.2 24.9 %copy-start.4 = (f32[512]{0:T(512)}, f32[512]{0:T(512)S(1)}, u32[]{:S(2)}) copy-start(f32[512]{0:T(512)S(1)} %broadcast_add_fusion) | copy-start | bytes 6148
  158.7 5.7 %copy-start.1 = (bf16[512,16384]{1,0:T(8,128)(2,1)}, bf16[512,16384]{1,0:T(8,128)(2,1)S(1)}, u32[]{:S(2)}) copy-start(bf16[512,16384]{1,0:T(8,128)(2,1)S(1)} %fusion.4) | copy-start | bytes 50331652
  164.5 4.4 %copy-start.3 = (bf16[16384,128]{1,0:T(8,128)(2,1)S(1)}, bf16[16384,128]{1,0:T(8,128)(2,1)}, u32[]{:S(2)}) copy-start(bf16[16384,128]{1,0:T(8,128)(2,1)} %param.9) | copy-start | bytes 12582916
  164.5 13.7 %copy-start.5 = (f32[144]{0:T(256)S(1)}, f32[144]{0:T(256)}, u32[]{:S(2)}) copy-start(f32[144]{0:T(256)} %param.11) | copy-start | bytes 1732
Sparse Core Ops, SparseCore 0:
  10.5 125.7 all-gather.4
  179.3 75.8 all-gather.6
where the time goes:
time: 266 us; the launch traced here: 265 us
  waiting for transfers between devices  142 us (53%)
  blocking collectives  58.2 us (22%)
  other arithmetic  21.4 us (8%)
  local copies, waits for them, and re-layouts  15.1 us (6%)
  between operations  15 us (6%)
  matrix products  13.7 us (5%)
    all_gather x1, waiting for transfers between devices, turned_gather(): whole = lax.all_gather(both, axis, axis=0, tiled=True)  72.5 us
    all_gather x1, waiting for transfers between devices, local(): lax.all_gather(hidden, 'tp', axis=1, tiled=True)  68.7 us
    all_gather x1, blocking collectives, local(): lax.all_gather(norm_gain[None, :].astype(jnp.bfloat16), 'tp', axis=1, til...  58.2 us
    unnamed x15, local copies, waits for them, and re-layouts  11.2 us
    dot_general x1, matrix products, local(): jnp.dot(full_payload, w_query, preferred_element_type=jnp.float32)  9.25 us
    reduce_sum x1, other arithmetic, local(): square_sum = jnp.sum(widened * widened, axis=1)  7.43 us
    reduce_max x1, other arithmetic, local(): row_scale = jnp.max(jnp.abs(normed), axis=1) + tiny_eps  6.23 us
    convert_element_type x1, other arithmetic, local(): full_payload = (normed / row_scale[:, None]).astype(jnp.bfloat16)  5.48 us
  transfers between devices with their start and end apart: 2, of which 2 were waited for; matrix products, arithmetic and copies ran while one was open for 2% of the time, Pallas kernels for 0%

commit v1 on v0

--- a/solution.py
+++ b/solution.py
@@ -12,11 +12,16 @@
 rope_base = 500000.0
 
 
+def all_by_exchange(array, mesh_axis, dim):
+    stack = jnp.stack([array] * lax.axis_size(mesh_axis))
+    return jnp.concatenate(lax.all_to_all(stack, mesh_axis, 0, 0), axis=dim)
+
+
 def turned_gather(arrays, axis, dims):
     turned = [jnp.moveaxis(a, dim, 0) for a, dim in zip(arrays, dims)]
     widths = [t[0].size for t in turned]
     both = jnp.concatenate([t.reshape(-1, w) for t, w in zip(turned, widths)], axis=1)
-    whole = lax.all_gather(both, axis, axis=0, tiled=True)
+    whole = all_by_exchange(both, axis, 0)
     blocks = jnp.split(whole, [sum(widths[:k]) for k in range(1, len(widths))], axis=1)
     return tuple(
         (

time: 266 us -> 251 us (0.944)
  waiting for transfers between devices: 142 us -> 116 us
  starting transfers between devices: 0.12 us -> 10.5 us
    all_gather x1 -> x0, waiting for transfers between devices: 72.5 us -> none  [turned_gather(): whole = lax.all_gather(both, axis, axis=0, tiled=True)]
    all_to_all x0 -> x1, waiting for transfers between devices: none -> 47 us  [all_by_exchange(): return jnp.concatenate(lax.all_to_all(stack, mesh_axis, 0, 0), axis=dim)]
    all_to_all x0 -> x1, starting transfers between devices: none -> 10.5 us  [all_by_exchange(): return jnp.concatenate(lax.all_to_all(stack, mesh_axis, 0, 0), axis=dim)]
where the time goes in v1:
time: 251 us; the launch traced here: 250 us
  waiting for transfers between devices  116 us (46%)
  blocking collectives  58.2 us (23%)
  other arithmetic  20.8 us (8%)
  local copies, waits for them, and re-layouts  15.2 us (6%)
  between operations  15 us (6%)
  matrix products  13.7 us (5%)
  starting transfers between devices  10.5 us (4%)
    all_gather x1, waiting for transfers between devices, local(): lax.all_gather(hidden, 'tp', axis=1, tiled=True)  68.7 us
    all_gather x1, blocking collectives, local(): lax.all_gather(norm_gain[None, :].astype(jnp.bfloat16), 'tp', axis=1, til...  58.2 us
    all_to_all x1, waiting for transfers between devices, all_by_exchange(): return jnp.concatenate(lax.all_to_all(stack, mesh_axis, 0, 0), axis=dim)  47 us
    unnamed x15, local copies, waits for them, and re-layouts  11.2 us
    all_to_all x1, starting transfers between devices, all_by_exchange(): return jnp.concatenate(lax.all_to_all(stack, mesh_axis, 0, 0), axis=dim)  10.5 us
    dot_general x1, matrix products, local(): jnp.dot(full_payload, w_query, preferred_element_type=jnp.float32)  9.26 us
    reduce_sum x1, other arithmetic, local(): square_sum = jnp.sum(widened * widened, axis=1)  7.43 us
    reduce_max x1, other arithmetic, local(): row_scale = jnp.max(jnp.abs(normed), axis=1) + tiny_eps  6.23 us
  transfers between devices with their start and end apart: 2, of which 2 were waited for; matrix products, arithmetic and copies ran while one was open for 2% of the time, Pallas kernels for 0%

profile of v1, /device:TPU:513, one launch (start us, length us, event | category | flops | bytes accessed | tf_op | source)
XLA Modules:
  0.0 249.7 jit_solution(6166466555624683161)
XLA Ops:
  7.2 0.0 copy-start
  7.2 0.1 all-gather.4.cloned.1.call-start
  7.3 0.7 all-gather.4.cloned.1.call-update
  8.0 0.7 convert_bitcast_fusion
  8.7 58.2 %all-gather.1 = bf16[128,1,128]{2,1,0:T(2,128)(2,1)S(1)} all-gather(bf16[1,1,128]{2,1,0:T(2,128)(2,1)S(1)} %convert_bitcast_fusion), channel_id=2, replica_groups=mesh['grp'=2,'tp'=128] {'tp'}, dimensions={0}, use_global_device_ids=true | all-gather | bytes 33024 | tf_op jit(solution)/shard_map/all_gather | solution.py:68
  66.9 0.1 mul.199
  67.6 68.7 %all-gather.4.cloned.1.call-done = bf16[512,16384]{1,0:T(8,128)(2,1)} async-done(((bf16[512,128]{1,0:T(8,128)(2,1)}), bf16[512,16384]{1,0:T(8,128)(2,1)}) %all-gather.4.cloned.1.call-update) | async-done | bytes 16777232 | tf_op jit(solution)/shard_map/all_gather | solution.py:67
  136.3 7.4 %fusion.5 = f32[512]{0:T(512)S(1)} fusion(bf16[512,16384]{1,0:T(8,128)(2,1)} %all-gather.4.cloned.1.call-done), kind=kLoop, calls=%fused_computation.7 | loop fusion | flops 25165312 | bytes 16779264 | tf_op jit(solution)/shard_map/reduce_sum | solution.py:73
  143.8 3.2 %copy-done.2 = bf16[512,16384]{1,0:T(8,128)(2,1)S(1)} copy-done((bf16[512,16384]{1,0:T(8,128)(2,1)S(1)}, bf16[512,16384]{1,0:T(8,128)(2,1)}, u32[]{:S(2)}) %copy-start.2) | copy-done | bytes 16777240
  147.0 6.2 %fusion.3 = f32[512]{0:T(512)S(1)} fusion(bf16[512,16384]{1,0:T(8,128)(2,1)S(1)} %copy-done.2, f32[16384]{0:T(1024)S(1)} %bitcast.34, f32[512]{0:T(512)S(1)} %add_rsqrt_fusion), kind=kLoop, calls=%fused_computation.5 | loop fusion | flops 41942528 | bytes 16846848 | tf_op jit(solution)/shard_map/reduce_max | solution.py:76
  153.2 0.0 copy-start.4
  153.2 5.5 %fusion.4 = bf16[512,16384]{1,0:T(8,128)(2,1)S(1)} fusion(bf16[512,16384]{1,0:T(8,128)(2,1)S(1)} %copy-done.2, f32[16384]{0:T(1024)S(1)} %bitcast.35, f32[512]{0:T(512)S(1)} %broadcast_add_fusion, f32[512]{0:T(512)S(1)} %add_rsqrt_fusion), kind=kLoop, calls=%fused_computation.6 | loop fusion | flops 41943040 | bytes 33624064 | tf_op jit(solution)/shard_map/convert_element_type | solution.py:77
  158.7 0.0 copy-start.1
  158.7 5.7 %copy-done.1 = bf16[512,16384]{1,0:T(8,128)(2,1)} copy-done((bf16[512,16384]{1,0:T(8,128)(2,1)}, bf16[512,16384]{1,0:T(8,128)(2,1)S(1)}, u32[]{:S(2)}) %copy-start.1) | copy-done | bytes 16777240
  164.5 0.0 copy-done
  164.5 4.4 %fusion.30 = f32[512,16]{0,1:T(8,128)S(1)} fusion(bf16[512,16384]{1,0:T(8,128)(2,1)S(1)} %fusion.4, bf16[16,16384]{1,0:T(8,128)(2,1)S(1)} %copy-done), kind=kOutput, calls=%fused_computation.64 | convolution fusion | flops 268435456 | bytes 17334272 | tf_op jit(solution)/shard_map/dot_general | solution.py:50
  168.9 9.3 %fusion.29 = f32[512,128]{0,1:T(8,128)S(1)} fusion(bf16[512,16384]{1,0:T(8,128)(2,1)} %copy-done.1, bf16[16384,128]{1,0:T(8,128)(2,1)S(1)} %copy-done.3), kind=kOutput, calls=%fused_computation.63 | convolution fusion | flops 2147483648 | bytes 21233664 | tf_op jit(solution)/shard_map/dot_general | solution.py:81
  178.2 0.1 fusion.6
  178.3 0.1 fusion.20
  178.6 1.6 stack.10
  180.2 10.5 %all-to-all-start = ((bf16[128,8,1024]{2,1,0:T(8,128)(2,1)}), bf16[128,8,1024]{2,1,0:T(8,128)(2,1)S(1)}, u32[]{:S(2)}, u32[]{:S(2)}) async-start(bf16[128,8,1024]{2,1,0:T(8,128)(2,1)} %stack.10), calls=%async_computation | async-start | bytes 4194304 | tf_op jit(solution)/shard_map/all_to_all | solution.py:17
  190.7 0.1 reshape.295
  190.8 0.2 fusion.27
  191.1 0.6 fusion.12
  191.7 0.1 copy.24
  191.8 0.1 convert_element_type.50
  191.9 0.8 copy.28
  192.6 1.6 constant_dynamic-slice_fusion
  194.2 47.0 %all-to-all-done = bf16[128,8,1024]{2,1,0:T(8,128)(2,1)S(1)} async-done(((bf16[128,8,1024]{2,1,0:T(8,128)(2,1)}), bf16[128,8,1024]{2,1,0:T(8,128)(2,1)S(1)}, u32[]{:S(2)}, u32[]{:S(2)}) %all-to-all-start) | async-done | bytes 2097184 | tf_op jit(solution)/shard_map/all_to_all | solution.py:17
  241.2 0.2 fusion.26
  241.4 0.8 copy.29
  242.1 0.8 copy.30
  (22 shorter events, 0.2 us)
Async XLA Ops:
  7.2 157.3 %copy-start = (bf16[16,16384]{1,0:T(8,128)(2,1)S(1)}, bf16[16,16384]{1,0:T(8,128)(2,1)}, u32[]{:S(2)}) copy-start(bf16[16,16384]{1,0:T(8,128)(2,1)} %param.10) | copy-start | bytes 1572868
  7.2 129.1 %all-gather.4.cloned.1.call-start = ((), (), s32[]{:S(2)}) async-start(), calls=%async_computation.1 | async-start | bytes 16908288 | tf_op jit(solution)/shard_map/all_gather | solution.py:67
  136.3 10.7 %copy-start.2 = (bf16[512,16384]{1,0:T(8,128)(2,1)S(1)}, bf16[512,16384]{1,0:T(8,128)(2,1)}, u32[]{:S(2)}) copy-start(bf16[512,16384]{1,0:T(8,128)(2,1)} %all-gather.4.cloned.1.call-done) | copy-start | bytes 50331652
  153.2 24.9 %copy-start.4 = (f32[512]{0:T(512)}, f32[512]{0:T(512)S(1)}, u32[]{:S(2)}) copy-start(f32[512]{0:T(512)S(1)} %broadcast_add_fusion) | copy-start | bytes 6148
  158.7 5.7 %copy-start.1 = (bf16[512,16384]{1,0:T(8,128)(2,1)}, bf16[512,16384]{1,0:T(8,128)(2,1)S(1)}, u32[]{:S(2)}) copy-start(bf16[512,16384]{1,0:T(8,128)(2,1)S(1)} %fusion.4) | copy-start | bytes 50331652
  164.5 4.4 %copy-start.3 = (bf16[16384,128]{1,0:T(8,128)(2,1)S(1)}, bf16[16384,128]{1,0:T(8,128)(2,1)}, u32[]{:S(2)}) copy-start(bf16[16384,128]{1,0:T(8,128)(2,1)} %param.9) | copy-start | bytes 12582916
  164.5 13.7 %copy-start.5 = (f32[144]{0:T(256)S(1)}, f32[144]{0:T(256)}, u32[]{:S(2)}) copy-start(f32[144]{0:T(256)} %param.11) | copy-start | bytes 1732
  180.2 61.0 %all-to-all-start = ((bf16[128,8,1024]{2,1,0:T(8,128)(2,1)}), bf16[128,8,1024]{2,1,0:T(8,128)(2,1)S(1)}, u32[]{:S(2)}, u32[]{:S(2)}) async-start(bf16[128,8,1024]{2,1,0:T(8,128)(2,1)} %stack.10), calls=%async_computation | async-start | bytes 4194304 | tf_op jit(solution)/shard_map/all_to_all | solution.py:17
Sparse Core Ops, SparseCore 0:
  10.5 125.7 all-gather.3
